TPU v7x, 32 devices: a whole 2x2x4 slice. The times are simulated.
32 devices in a mesh: groups: 2 (over x), samples: 16 (over z, y, core).
Axes of the slice: x: 2, y: 2, z: 4, core: 2. Of those that a mesh axis runs over, the one named last changes fastest.
Arguments:
- terms: float32 [1048576, 64], P(('groups', 'samples')), parts along dimension 0
- coefficients: float32 [64, 256], replicated, may hold values from -1.5 to 1.5
- counts: int32 [512], P('groups'), parts along dimension 0, may hold values from 1 to 4095, as said below
- labels: int32 [1048576], P(('groups', 'samples')), parts along dimension 0, may hold values from 0 to 255, as said below
- f_start: float32 [512], P('groups'), parts along dimension 0, may hold values from -8 to 8
Outputs:
- free: float32 [512], P('groups'), parts along dimension 0
- intersection: float32 [512, 256], P(('groups', 'samples')), parts along dimension 0
- anchor_mix: float32 [512, 256], P(('groups', 'samples')), parts along dimension 0
- term_means: float32 [512, 64], P(('groups', 'samples')), parts along dimension 0
There are 2 independent parts, one for each index of `groups`. A program takes and returns all parts, laid end to end along the dimension named above; an argument that names none is the same for every part. Nothing has to cross between parts.
Inputs may be any that keep to these rules, and one draw needn't show every extreme that they name: counts sum to 524288. `labels`: exactly counts[k] snapshots carry the label k.
All inputs are finite; a program needn't handle non-finite values.
Results may differ from a plain program's by a relative error of at most 0.0003.
Values sent between devices are 32-bit elements; how exact they have to be, the bound alone decides.
A program may use at most 128 MiB of HBM per device.

v0:
```python
import jax
import jax.numpy as jnp
from jax import lax
from jax.sharding import PartitionSpec as P

ITERS = 4


def energies(block, coefficients):
    return jnp.dot(
        block, coefficients, precision=lax.Precision.HIGHEST, preferred_element_type=jnp.float32
    )


def denominator(energy, free_now, log_counts):
    shifted = log_counts[None, :] + free_now[None, :] - energy
    top = jnp.max(shifted, axis=1, keepdims=True)
    return top[:, 0] + jnp.log(jnp.sum(jnp.exp(shifted - top), axis=1))


def local(terms, coefficients, counts, labels, f_start):
    rows = terms.shape[0]
    states = coefficients.shape[1]
    block_rows = min(4096, rows)
    blocks = terms.reshape(rows // block_rows, block_rows, terms.shape[1])
    label_blocks = labels.reshape(rows // block_rows, block_rows)
    log_counts = jnp.log(counts.astype(jnp.float32))
    scaled_counts = counts.astype(jnp.float32)
    free_now = f_start
    for step in range(ITERS):

        def accumulate(carry, block):
            peak, total = carry
            energy = energies(block, coefficients)
            denom = denominator(energy, free_now, log_counts)
            logw = -energy - denom[:, None]
            new_peak = jnp.maximum(peak, jnp.max(logw, axis=0))
            total = total * jnp.exp(peak - new_peak) + jnp.sum(
                jnp.exp(logw - new_peak[None, :]), axis=0
            )
            return ((new_peak, total), None)

        init = (jnp.full((states,), -1e30, jnp.float32), jnp.zeros((states,), jnp.float32))
        (peak, total), _ = lax.scan(accumulate, init, blocks)
        highest = lax.pmax(peak, "samples")
        total = lax.psum(total * jnp.exp(peak - highest), "samples")
        peak = highest
        updated = -(peak + jnp.log(total))
        free_now = updated - updated[0]
    state_ids = jnp.arange(states, dtype=jnp.int32)

    def diagnose(carry, pair):
        over, anchor, term_sum, weight_sum = carry
        block, label_block = pair
        energy = energies(block, coefficients)
        denom = denominator(energy, free_now, log_counts)
        weight = jnp.exp(free_now[None, :] - energy - denom[:, None])
        over = over + jnp.dot(
            weight.T,
            weight * scaled_counts[None, :],
            precision=lax.Precision.HIGHEST,
            preferred_element_type=jnp.float32,
        )
        onehot = (label_block[:, None] == state_ids[None, :]).astype(jnp.float32)
        anchor = anchor + jnp.dot(
            onehot.T, weight, precision=lax.Precision.HIGHEST, preferred_element_type=jnp.float32
        )
        term_sum = term_sum + jnp.dot(
            weight.T, block, precision=lax.Precision.HIGHEST, preferred_element_type=jnp.float32
        )
        weight_sum = weight_sum + jnp.sum(weight, axis=0)
        return ((over, anchor, term_sum, weight_sum), None)

    init = (
        jnp.zeros((states, states), jnp.float32),
        jnp.zeros((states, states), jnp.float32),
        jnp.zeros((states, terms.shape[1]), jnp.float32),
        jnp.zeros((states,), jnp.float32),
    )
    (over, anchor, term_sum, weight_sum), _ = lax.scan(diagnose, init, (blocks, label_blocks))
    over, anchor, term_sum, weight_sum = lax.psum((over, anchor, term_sum, weight_sum), "samples")
    owned = states // lax.axis_size("samples")
    first_row = lax.axis_index("samples") * owned
    over = lax.dynamic_slice_in_dim(over, first_row, owned, 0)
    anchor = lax.dynamic_slice_in_dim(anchor, first_row, owned, 0)
    term_sum = lax.dynamic_slice_in_dim(term_sum, first_row, owned, 0)
    weight_sum = lax.dynamic_slice_in_dim(weight_sum, first_row, owned, 0)
    return (free_now, over, anchor, term_sum / weight_sum[:, None])


def solution(mesh):
    return jax.shard_map(
        local,
        mesh=mesh,
        in_specs=(
            P(("groups", "samples"), None),
            P(),
            P("groups"),
            P(("groups", "samples")),
            P("groups"),
        ),
        out_specs=(
            P("groups"),
            P(("groups", "samples"), None),
            P(("groups", "samples"), None),
            P(("groups", "samples"), None),
        ),
        check_vma=False,
    )
```

profile of v0, /device:TPU:0, one launch (start us, length us, event | category | flops | bytes accessed | tf_op | source)
XLA Modules:
  0.0 897.7 jit_solution(15325472563780318898)
XLA Ops:
  7.4 12.3 %copy.9 = f32[32768,64]{1,0:T(8,128)} copy(f32[32768,64]{0,1:T(8,128)} %param.15) | data formatting | bytes 16777216 | tf_op args[0]
  19.7 84.8 %while.79 = (s32[]{:T(128)}, f32[256]{0:T(256)S(1)}, f32[256]{0:T(256)S(1)}, f32[8,4096,64]{2,1,0:T(8,128)}, f32[64,256]{1,0:T(8,128)S(1)}, /*index=5*/f32[1,256]{1,0:T(1,128)S(1)}, s32[]{:T(128)}, s32[]{:T(128)}) while((s32[]{:T(128)}, f32[256]{0:T(256)S(1)}, f32[256]{0:T(256)S(1)}, f32[8,4096,64]{2,1,0:T(8,128)}, ...), condition=%wide.region_5.6_spmd.clone, body=%wide.region_0.5_spmd.clone.sunk | while | flops 817886464 | bytes 35864184 | solution.py:44
  19.7 5.2 subtract_reduce_fusion.10
  30.3 5.2 subtract_reduce_fusion.10
  51.5 5.2 subtract_reduce_fusion.10
  62.1 5.2 subtract_reduce_fusion.10
  83.3 5.2 subtract_reduce_fusion.10
  93.9 5.2 subtract_reduce_fusion.10
  104.5 35.0 %pmax.28 = f32[256]{0:T(256)S(1)} all-reduce(f32[256]{0:T(256)S(1)} %get-tuple-element.470), channel_id=1, replica_groups=mesh['groups'=2,'samples'=16] {'samples'}, use_global_device_ids=true, to_apply=%region_6.7 | all-reduce | flops 256 | bytes 2048 | tf_op jit(solution)/shard_map/pmax | solution.py:45
  139.4 29.5 %psum.56 = f32[256]{0:T(256)S(1)} all-reduce(f32[256]{0:T(256)S(1)} %exponential_multiply_fusion.3), channel_id=1, replica_groups=mesh['groups'=2,'samples'=16] {'samples'}, use_global_device_ids=true, to_apply=%region_7.8 | all-reduce | flops 256 | bytes 2048 | tf_op jit(solution)/shard_map/psum | solution.py:46
  170.0 84.8 %while.80 = (s32[]{:T(128)}, f32[256]{0:T(256)S(1)}, f32[256]{0:T(256)S(1)}, f32[8,4096,64]{2,1,0:T(8,128)}, f32[64,256]{1,0:T(8,128)S(1)}, /*index=5*/f32[1,256]{1,0:T(1,128)S(1)}, s32[]{:T(128)}, s32[]{:T(128)}) while((s32[]{:T(128)}, f32[256]{0:T(256)S(1)}, f32[256]{0:T(256)S(1)}, f32[8,4096,64]{2,1,0:T(8,128)}, ...), condition=%wide.region_13.14_spmd.clone, body=%wide.region_8.13_spmd.clone.sunk | while | flops 817886464 | bytes 35864184 | solution.py:44
  191.2 5.2 subtract_reduce_fusion.11
  233.6 5.2 subtract_reduce_fusion.11
  254.8 29.5 %pmax.29 = f32[256]{0:T(256)S(1)} all-reduce(f32[256]{0:T(256)S(1)} %get-tuple-element.472), channel_id=1, replica_groups=mesh['groups'=2,'samples'=16] {'samples'}, use_global_device_ids=true, to_apply=%region_14.15 | all-reduce | flops 256 | bytes 2048 | tf_op jit(solution)/shard_map/pmax | solution.py:45
  284.3 29.7 %psum.57 = f32[256]{0:T(256)S(1)} all-reduce(f32[256]{0:T(256)S(1)} %exponential_multiply_fusion.2), channel_id=1, replica_groups=mesh['groups'=2,'samples'=16] {'samples'}, use_global_device_ids=true, to_apply=%region_15.16 | all-reduce | flops 256 | bytes 2048 | tf_op jit(solution)/shard_map/psum | solution.py:46
  315.1 84.8 %while.81 = (s32[]{:T(128)}, f32[256]{0:T(256)S(1)}, f32[256]{0:T(256)S(1)}, f32[8,4096,64]{2,1,0:T(8,128)}, f32[64,256]{1,0:T(8,128)S(1)}, /*index=5*/f32[1,256]{1,0:T(1,128)S(1)}, s32[]{:T(128)}, s32[]{:T(128)}) while((s32[]{:T(128)}, f32[256]{0:T(256)S(1)}, f32[256]{0:T(256)S(1)}, f32[8,4096,64]{2,1,0:T(8,128)}, ...), condition=%wide.region_21.22_spmd.clone, body=%wide.region_16.21_spmd.clone.sunk | while | flops 817886464 | bytes 35864184 | solution.py:44
  399.9 29.5 %pmax.30 = f32[256]{0:T(256)S(1)} all-reduce(f32[256]{0:T(256)S(1)} %get-tuple-element.474), channel_id=1, replica_groups=mesh['groups'=2,'samples'=16] {'samples'}, use_global_device_ids=true, to_apply=%region_22.23 | all-reduce | flops 256 | bytes 2048 | tf_op jit(solution)/shard_map/pmax | solution.py:45
  429.4 29.5 %psum.58 = f32[256]{0:T(256)S(1)} all-reduce(f32[256]{0:T(256)S(1)} %exponential_multiply_fusion.1), channel_id=1, replica_groups=mesh['groups'=2,'samples'=16] {'samples'}, use_global_device_ids=true, to_apply=%region_23.24 | all-reduce | flops 256 | bytes 2048 | tf_op jit(solution)/shard_map/psum | solution.py:46
  460.1 84.9 %while.82 = (s32[]{:T(128)}, f32[256]{0:T(256)S(1)}, f32[256]{0:T(256)S(1)}, f32[8,4096,64]{2,1,0:T(8,128)}, f32[64,256]{1,0:T(8,128)S(1)}, /*index=5*/f32[1,256]{1,0:T(1,128)S(1)}, s32[]{:T(128)}, s32[]{:T(128)}) while((s32[]{:T(128)}, f32[256]{0:T(256)S(1)}, f32[256]{0:T(256)S(1)}, f32[8,4096,64]{2,1,0:T(8,128)}, ...), condition=%wide.region_29.30_spmd.clone, body=%wide.region_24.29_spmd.clone.sunk | while | flops 817886464 | bytes 35864184 | solution.py:44
  460.1 5.2 subtract_reduce_fusion.13
  470.7 5.2 subtract_reduce_fusion.13
  481.3 5.2 subtract_reduce_fusion.13
  491.9 5.2 subtract_reduce_fusion.13
  502.5 5.2 subtract_reduce_fusion.13
  513.1 5.2 subtract_reduce_fusion.13
  523.7 5.2 subtract_reduce_fusion.13
  534.3 5.2 subtract_reduce_fusion.13
  544.9 29.5 %pmax.31 = f32[256]{0:T(256)S(1)} all-reduce(f32[256]{0:T(256)S(1)} %get-tuple-element.476), channel_id=1, replica_groups=mesh['groups'=2,'samples'=16] {'samples'}, use_global_device_ids=true, to_apply=%region_30.31 | all-reduce | flops 256 | bytes 2048 | tf_op jit(solution)/shard_map/pmax | solution.py:45
  574.4 29.5 %psum.59 = f32[256]{0:T(256)S(1)} all-reduce(f32[256]{0:T(256)S(1)} %exponential_multiply_fusion), channel_id=1, replica_groups=mesh['groups'=2,'samples'=16] {'samples'}, use_global_device_ids=true, to_apply=%region_31.32 | all-reduce | flops 256 | bytes 2048 | tf_op jit(solution)/shard_map/psum | solution.py:46
  605.2 192.2 %while.83 = (s32[]{:T(128)}, f32[256,256]{1,0:T(8,128)S(1)}, f32[256,256]{1,0:T(8,128)S(1)}, f32[256,64]{0,1:T(8,128)S(1)}, f32[256]{0:T(256)S(1)}, /*index=5*/f...) while((s32[]{:T(128)}, f32[256,256]{1,0:T(8,128)S(1)}, ...), condition=%wide.region_36.37_spmd.clone, body=%wide.region_32.36_spmd.clone.sunk | while | flops 8073277952 | bytes 64385216 | solution.py:80
  605.4 5.3 subtract_reduce_fusion.14
  613.5 7.2 fusion.106
  629.4 5.3 subtract_reduce_fusion.14
  637.5 7.2 fusion.106
  653.4 5.3 subtract_reduce_fusion.14
  661.5 7.2 fusion.106
  677.4 5.3 subtract_reduce_fusion.14
  685.5 7.2 fusion.106
  701.4 5.3 subtract_reduce_fusion.14
  709.5 7.2 fusion.106
  725.4 5.3 subtract_reduce_fusion.14
  733.5 7.2 fusion.106
  749.4 5.3 subtract_reduce_fusion.14
  757.5 7.2 fusion.106
  773.4 5.3 subtract_reduce_fusion.14
  781.5 7.2 fusion.106
  798.2 29.7 %psum.63 = f32[256]{0:T(256)S(1)} all-reduce(f32[256]{0:T(256)S(1)} %get-tuple-element.481), channel_id=1, replica_groups=mesh['groups'=2,'samples'=16] {'samples'}, use_global_device_ids=true, to_apply=%region_40.41 | all-reduce | flops 256 | bytes 2048 | tf_op jit(solution)/shard_map/psum | solution.py:81
  828.0 59.8 %all-reduce.3.cloned.1.call-done = (f32[256,256]{1,0:T(8,128)}, f32[256,256]{1,0:T(8,128)}, f32[256,64]{1,0:T(8,128)}) async-done(((f32[256,256]{1,0:T(8,128)}, f32[256,256]{1,0:T(8,128)}, f32[256,64]{1,0:T(8,128)}), (f32[256,256]{1,0:T(8,128)}, f32[256,256]{1,0:T(8,128)}, f32[256,64]{1,0:T(8,128)})) %all-reduce.3.cloned.1.call-update) | async-done | bytes 589840 | tf_op jit(solution)/shard_map/psum | solution.py:81
  (443 shorter events, 353.1 us)
Async XLA Ops:
  7.2 880.6 %all-reduce.3.cloned.1.call-start = ((), (), s32[]{:S(2)}) async-start(), calls=%async_computation | async-start | bytes 1310720 | tf_op jit(solution)/shard_map/psum | solution.py:81
  7.3 12.3 %copy-start.11 = (s32[256]{0:T(256)S(1)}, s32[256]{0:T(256)}, u32[]{:S(2)}) copy-start(s32[256]{0:T(256)} %param.17) | copy-start | bytes 3076
  7.3 12.3 %copy-start.12 = (f32[256]{0:T(256)S(1)}, f32[256]{0:T(256)}, u32[]{:S(2)}) copy-start(f32[256]{0:T(256)} %param.19) | copy-start | bytes 3076
  7.3 12.3 %copy-start.6 = (f32[64,256]{1,0:T(8,128)S(1)}, f32[64,256]{1,0:T(8,128)}, u32[]{:S(2)}) copy-start(f32[64,256]{1,0:T(8,128)} %param.16) | copy-start | bytes 196612
  24.8 1.9 copy-start.2
  35.4 1.9 copy-start.2
  46.0 1.9 copy-start.2
  56.6 1.9 copy-start.2
  67.2 1.9 copy-start.2
  77.8 1.9 copy-start.2
  88.4 1.9 copy-start.2
  99.0 1.9 copy-start.2
  175.2 1.9 copy-start.3
  185.8 1.9 copy-start.3
  196.4 1.9 copy-start.3
  207.0 1.9 copy-start.3
  217.6 1.9 copy-start.3
  228.2 1.9 copy-start.3
  238.8 1.9 copy-start.3
  249.4 1.9 copy-start.3
  320.3 1.9 copy-start.4
  330.9 1.9 copy-start.4
  341.5 1.9 copy-start.4
  352.1 1.9 copy-start.4
  362.7 1.9 copy-start.4
  373.3 1.9 copy-start.4
  383.9 1.9 copy-start.4
  394.5 1.9 copy-start.4
  460.1 145.0 %copy-start.9 = (s32[32768]{0:T(1024)S(1)}, s32[32768]{0:T(1024)}, u32[]{:S(2)}) copy-start(s32[32768]{0:T(1024)} %param.18) | copy-start | bytes 393220
  465.3 1.9 copy-start.5
  475.9 1.9 copy-start.5
  486.5 1.9 copy-start.5
  497.1 1.9 copy-start.5
  507.7 1.9 copy-start.5
  518.3 1.9 copy-start.5
  528.9 1.9 copy-start.5
  539.5 1.9 copy-start.5
  613.5 7.3 copy-start.1
  637.5 7.3 copy-start.1
  658.7 1.9 copy-start
  661.5 7.3 copy-start.1
  682.7 1.9 copy-start
  685.5 7.3 copy-start.1
  709.5 7.3 copy-start.1
  733.5 7.3 copy-start.1
  757.5 7.3 copy-start.1
  781.5 7.3 copy-start.1
  797.4 93.1 %copy-start.10 = (f32[256]{0:T(256)}, f32[256]{0:T(256)S(1)}, u32[]{:S(2)}) copy-start(f32[256]{0:T(256)S(1)} %get-tuple-element.1079) | copy-start | bytes 3076
  (8 other events, 13.2 us)
Sparse Core Ops, SparseCore 0:
  798.4 89.3 all-reduce.2
where the time goes:
time: 908 us; the launch traced here: 898 us
  matrix products  335 us (37%)
  blocking collectives  271 us (30%)
  other arithmetic  176 us (19%)
  waiting for transfers between devices  59.8 us (7%)
  local copies, waits for them, and re-layouts  38.3 us (4%)
  between operations  14.7 us (2%)
    dot_general x40, matrix products, energies(): jnp.dot(block, coefficients, precision=lax.Precision.HIGHEST, preferred_e...  208 us
    pmax x4, blocking collectives, local(): highest = lax.pmax(peak, 'samples')  123 us
    psum x4, blocking collectives, local(): total = lax.psum(total * jnp.exp(peak - highest), 'samples')  118 us
    reduce_sum x32, other arithmetic, accumulate(): jnp.sum(jnp.exp(logw - new_peak[None, :]), axis=0)  87 us
    psum x1, waiting for transfers between devices, local(): lax.psum((over, anchor, term_sum, weight_sum), 'samples')  59.8 us
    dot_general x8, matrix products, diagnose(): jnp.dot(weight.T, block, precision=lax.Precision.HIGHEST, preferred_eleme...  57.9 us
    reduce_sum x40, other arithmetic, denominator(): return top[:, 0] + jnp.log(jnp.sum(jnp.exp(shifted - top), axis=1))  54.4 us
    dot_general x8, matrix products, diagnose(): jnp.dot(weight.T, weight * scaled_counts[None, :], precision=lax.Precisio...  39 us
  transfers between devices with their start and end apart: 1, of which 1 were waited for; matrix products, arithmetic and copies ran while one was open for 0% of the time, Pallas kernels for 0%

commit v1 on v0

--- a/solution.py
+++ b/solution.py
@@ -43,7 +43,7 @@
         init = (jnp.full((states,), -1e30, jnp.float32), jnp.zeros((states,), jnp.float32))
         (peak, total), _ = lax.scan(accumulate, init, blocks)
         highest = lax.pmax(peak, "samples")
-        total = lax.psum(total * jnp.exp(peak - highest), "samples")
+        total = jnp.sum(lax.all_gather(total * jnp.exp(peak - highest), "samples"), axis=0)
         peak = highest
         updated = -(peak + jnp.log(total))
         free_now = updated - updated[0]

time: 908 us -> 866 us (0.954)
  blocking collectives: 271 us -> 230 us
    psum x4 -> x0, blocking collectives: 118 us -> none  [local(): total = lax.psum(total * jnp.exp(peak - highest), 'samples')]
    all_gather x0 -> x4, blocking collectives: none -> 68.8 us  [local(): lax.all_gather(total * jnp.exp(peak - highest), 'samples')]
where the time goes in v1:
time: 866 us; the launch traced here: 856 us
  matrix products  335 us (39%)
  blocking collectives  230 us (27%)
  other arithmetic  176 us (20%)
  waiting for transfers between devices  59.3 us (7%)
  local copies, waits for them, and re-layouts  38.3 us (4%)
  between operations  14.7 us (2%)
    dot_general x40, matrix products, energies(): jnp.dot(block, coefficients, precision=lax.Precision.HIGHEST, preferred_e...  208 us
    pmax x4, blocking collectives, local(): highest = lax.pmax(peak, 'samples')  129 us
    reduce_sum x32, other arithmetic, accumulate(): jnp.sum(jnp.exp(logw - new_peak[None, :]), axis=0)  87 us
    all_gather x4, blocking collectives, local(): lax.all_gather(total * jnp.exp(peak - highest), 'samples')  68.8 us
    psum x1, waiting for transfers between devices, local(): lax.psum((over, anchor, term_sum, weight_sum), 'samples')  59.3 us
    dot_general x8, matrix products, diagnose(): jnp.dot(weight.T, block, precision=lax.Precision.HIGHEST, preferred_eleme...  58 us
    reduce_sum x40, other arithmetic, denominator(): return top[:, 0] + jnp.log(jnp.sum(jnp.exp(shifted - top), axis=1))  54.4 us
    dot_general x8, matrix products, diagnose(): jnp.dot(weight.T, weight * scaled_counts[None, :], precision=lax.Precisio...  39 us
  transfers between devices with their start and end apart: 1, of which 1 were waited for; matrix products, arithmetic and copies ran while one was open for 0% of the time, Pallas kernels for 0%

profile of v1, /device:TPU:0, one launch (start us, length us, event | category | flops | bytes accessed | tf_op | source)
XLA Modules:
  0.0 855.8 jit_solution(17649505619400609874)
XLA Ops:
  7.4 12.3 %copy.11 = f32[32768,64]{1,0:T(8,128)} copy(f32[32768,64]{0,1:T(8,128)} %param.15) | data formatting | bytes 16777216 | tf_op args[0]
  19.7 84.8 %while.79 = (s32[]{:T(128)}, f32[256]{0:T(256)S(1)}, f32[256]{0:T(256)S(1)}, f32[8,4096,64]{2,1,0:T(8,128)}, f32[64,256]{1,0:T(8,128)S(1)}, /*index=5*/f32[1,256]{1,0:T(1,128)S(1)}, s32[]{:T(128)}, s32[]{:T(128)}) while((s32[]{:T(128)}, f32[256]{0:T(256)S(1)}, f32[256]{0:T(256)S(1)}, f32[8,4096,64]{2,1,0:T(8,128)}, ...), condition=%wide.region_5.6_spmd.clone, body=%wide.region_0.5_spmd.clone.sunk | while | flops 817886464 | bytes 35864184 | solution.py:44
  19.7 5.2 subtract_reduce_fusion.10
  30.3 5.2 subtract_reduce_fusion.10
  51.5 5.2 subtract_reduce_fusion.10
  62.1 5.2 subtract_reduce_fusion.10
  93.9 5.2 subtract_reduce_fusion.10
  104.5 35.0 %pmax.28 = f32[256]{0:T(256)S(1)} all-reduce(f32[256]{0:T(256)S(1)} %get-tuple-element.470), channel_id=1, replica_groups=mesh['groups'=2,'samples'=16] {'samples'}, use_global_device_ids=true, to_apply=%region_6.7 | all-reduce | flops 256 | bytes 2048 | tf_op jit(solution)/shard_map/pmax | solution.py:45
  139.4 17.2 %all-gather.4 = f32[16,1,256]{2,1,0:T(1,128)S(1)} all-gather(f32[1,1,256]{2,1,0:T(1,128)S(1)} %bitcast.105), channel_id=2, replica_groups=mesh['groups'=2,'samples'=16] {'samples'}, dimensions={0}, use_global_device_ids=true | all-gather | bytes 17408 | tf_op jit(solution)/shard_map/all_gather | solution.py:46
  157.7 84.8 %while.80 = (s32[]{:T(128)}, f32[256]{0:T(256)S(1)}, f32[256]{0:T(256)S(1)}, f32[8,4096,64]{2,1,0:T(8,128)}, f32[64,256]{1,0:T(8,128)S(1)}, /*index=5*/f32[1,256]{1,0:T(1,128)S(1)}, s32[]{:T(128)}, s32[]{:T(128)}) while((s32[]{:T(128)}, f32[256]{0:T(256)S(1)}, f32[256]{0:T(256)S(1)}, f32[8,4096,64]{2,1,0:T(8,128)}, ...), condition=%wide.region_13.14_spmd.clone, body=%wide.region_8.13_spmd.clone.sunk | while | flops 817886464 | bytes 35864184 | solution.py:44
  189.5 5.2 subtract_reduce_fusion.11
  210.7 5.2 subtract_reduce_fusion.11
  242.5 31.4 %pmax.29 = f32[256]{0:T(256)S(1)} all-reduce(f32[256]{0:T(256)S(1)} %get-tuple-element.472), channel_id=1, replica_groups=mesh['groups'=2,'samples'=16] {'samples'}, use_global_device_ids=true, to_apply=%region_14.15 | all-reduce | flops 256 | bytes 2048 | tf_op jit(solution)/shard_map/pmax | solution.py:45
  273.9 17.3 %all-gather.5 = f32[16,1,256]{2,1,0:T(1,128)S(1)} all-gather(f32[1,1,256]{2,1,0:T(1,128)S(1)} %bitcast.106), channel_id=3, replica_groups=mesh['groups'=2,'samples'=16] {'samples'}, dimensions={0}, use_global_device_ids=true | all-gather | bytes 17408 | tf_op jit(solution)/shard_map/all_gather | solution.py:46
  292.5 84.8 %while.81 = (s32[]{:T(128)}, f32[256]{0:T(256)S(1)}, f32[256]{0:T(256)S(1)}, f32[8,4096,64]{2,1,0:T(8,128)}, f32[64,256]{1,0:T(8,128)S(1)}, /*index=5*/f32[1,256]{1,0:T(1,128)S(1)}, s32[]{:T(128)}, s32[]{:T(128)}) while((s32[]{:T(128)}, f32[256]{0:T(256)S(1)}, f32[256]{0:T(256)S(1)}, f32[8,4096,64]{2,1,0:T(8,128)}, ...), condition=%wide.region_21.22_spmd.clone, body=%wide.region_16.21_spmd.clone.sunk | while | flops 817886464 | bytes 35864184 | solution.py:44
  292.5 5.2 subtract_reduce_fusion.12
  377.2 31.4 %pmax.30 = f32[256]{0:T(256)S(1)} all-reduce(f32[256]{0:T(256)S(1)} %get-tuple-element.474), channel_id=1, replica_groups=mesh['groups'=2,'samples'=16] {'samples'}, use_global_device_ids=true, to_apply=%region_22.23 | all-reduce | flops 256 | bytes 2048 | tf_op jit(solution)/shard_map/pmax | solution.py:45
  408.7 17.2 %all-gather.6 = f32[16,1,256]{2,1,0:T(1,128)S(1)} all-gather(f32[1,1,256]{2,1,0:T(1,128)S(1)} %bitcast.107), channel_id=4, replica_groups=mesh['groups'=2,'samples'=16] {'samples'}, dimensions={0}, use_global_device_ids=true | all-gather | bytes 17408 | tf_op jit(solution)/shard_map/all_gather | solution.py:46
  427.1 84.8 %while.82 = (s32[]{:T(128)}, f32[256]{0:T(256)S(1)}, f32[256]{0:T(256)S(1)}, f32[8,4096,64]{2,1,0:T(8,128)}, f32[64,256]{1,0:T(8,128)S(1)}, /*index=5*/f32[1,256]{1,0:T(1,128)S(1)}, s32[]{:T(128)}, s32[]{:T(128)}) while((s32[]{:T(128)}, f32[256]{0:T(256)S(1)}, f32[256]{0:T(256)S(1)}, f32[8,4096,64]{2,1,0:T(8,128)}, ...), condition=%wide.region_29.30_spmd.clone, body=%wide.region_24.29_spmd.clone.sunk | while | flops 817886464 | bytes 35864184 | solution.py:44
  427.1 5.2 subtract_reduce_fusion.13
  437.7 5.2 subtract_reduce_fusion.13
  448.3 5.2 subtract_reduce_fusion.13
  458.9 5.2 subtract_reduce_fusion.13
  469.5 5.2 subtract_reduce_fusion.13
  480.1 5.2 subtract_reduce_fusion.13
  490.7 5.2 subtract_reduce_fusion.13
  501.3 5.2 subtract_reduce_fusion.13
  511.9 31.4 %pmax.31 = f32[256]{0:T(256)S(1)} all-reduce(f32[256]{0:T(256)S(1)} %get-tuple-element.476), channel_id=1, replica_groups=mesh['groups'=2,'samples'=16] {'samples'}, use_global_device_ids=true, to_apply=%region_30.31 | all-reduce | flops 256 | bytes 2048 | tf_op jit(solution)/shard_map/pmax | solution.py:45
  543.3 17.2 %all-gather.7 = f32[16,1,256]{2,1,0:T(1,128)S(1)} all-gather(f32[1,1,256]{2,1,0:T(1,128)S(1)} %bitcast.108), channel_id=5, replica_groups=mesh['groups'=2,'samples'=16] {'samples'}, dimensions={0}, use_global_device_ids=true | all-gather | bytes 17408 | tf_op jit(solution)/shard_map/all_gather | solution.py:46
  561.8 192.2 %while.83 = (s32[]{:T(128)}, f32[256,256]{1,0:T(8,128)S(1)}, f32[256,256]{1,0:T(8,128)S(1)}, f32[256,64]{0,1:T(8,128)S(1)}, f32[256]{0:T(256)S(1)}, /*index=5*/f...) while((s32[]{:T(128)}, f32[256,256]{1,0:T(8,128)S(1)}, ...), condition=%wide.region_36.37_spmd.clone, body=%wide.region_32.36_spmd.clone.sunk | while | flops 8073277952 | bytes 64385216 | solution.py:80
  562.0 5.3 subtract_reduce_fusion.14
  570.1 7.2 fusion.106
  586.0 5.3 subtract_reduce_fusion.14
  594.1 7.2 fusion.106
  610.0 5.3 subtract_reduce_fusion.14
  618.1 7.2 fusion.106
  634.0 5.3 subtract_reduce_fusion.14
  642.1 7.2 fusion.106
  658.0 5.3 subtract_reduce_fusion.14
  666.1 7.2 fusion.106
  682.0 5.3 subtract_reduce_fusion.14
  690.1 7.2 fusion.106
  706.0 5.3 subtract_reduce_fusion.14
  714.1 7.2 fusion.106
  730.0 5.3 subtract_reduce_fusion.14
  738.1 7.2 fusion.106
  754.9 31.5 %psum.31 = f32[256]{0:T(256)S(1)} all-reduce(f32[256]{0:T(256)S(1)} %get-tuple-element.481), channel_id=1, replica_groups=mesh['groups'=2,'samples'=16] {'samples'}, use_global_device_ids=true, to_apply=%region_40.41 | all-reduce | flops 256 | bytes 2048 | tf_op jit(solution)/shard_map/psum | solution.py:81
  786.5 59.3 %all-reduce.3.cloned.1.call-done = (f32[256,256]{1,0:T(8,128)}, f32[256,256]{1,0:T(8,128)}, f32[256,64]{1,0:T(8,128)}) async-done(((f32[256,256]{1,0:T(8,128)}, f32[256,256]{1,0:T(8,128)}, f32[256,64]{1,0:T(8,128)}), (f32[256,256]{1,0:T(8,128)}, f32[256,256]{1,0:T(8,128)}, f32[256,64]{1,0:T(8,128)})) %all-reduce.3.cloned.1.call-update) | async-done | bytes 589840 | tf_op jit(solution)/shard_map/psum | solution.py:81
  (447 shorter events, 353.3 us)
Async XLA Ops:
  7.2 838.7 %all-reduce.3.cloned.1.call-start = ((), (), s32[]{:S(2)}) async-start(), calls=%async_computation | async-start | bytes 1310720 | tf_op jit(solution)/shard_map/psum | solution.py:81
  7.3 12.3 %copy-start.11 = (s32[256]{0:T(256)S(1)}, s32[256]{0:T(256)}, u32[]{:S(2)}) copy-start(s32[256]{0:T(256)} %param.17) | copy-start | bytes 3076
  7.3 12.3 %copy-start.12 = (f32[256]{0:T(256)S(1)}, f32[256]{0:T(256)}, u32[]{:S(2)}) copy-start(f32[256]{0:T(256)} %param.19) | copy-start | bytes 3076
  7.3 12.3 %copy-start.6 = (f32[64,256]{1,0:T(8,128)S(1)}, f32[64,256]{1,0:T(8,128)}, u32[]{:S(2)}) copy-start(f32[64,256]{1,0:T(8,128)} %param.16) | copy-start | bytes 196612
  24.8 1.9 copy-start.2
  35.4 1.9 copy-start.2
  46.0 1.9 copy-start.2
  56.6 1.9 copy-start.2
  67.2 1.9 copy-start.2
  77.8 1.9 copy-start.2
  88.4 1.9 copy-start.2
  99.0 1.9 copy-start.2
  162.9 1.9 copy-start.3
  173.5 1.9 copy-start.3
  184.1 1.9 copy-start.3
  194.7 1.9 copy-start.3
  205.3 1.9 copy-start.3
  215.9 1.9 copy-start.3
  226.5 1.9 copy-start.3
  237.1 1.9 copy-start.3
  297.7 1.9 copy-start.4
  308.3 1.9 copy-start.4
  318.9 1.9 copy-start.4
  329.5 1.9 copy-start.4
  340.0 1.9 copy-start.4
  350.6 1.9 copy-start.4
  361.2 1.9 copy-start.4
  371.8 1.9 copy-start.4
  427.0 134.7 %copy-start.9 = (s32[32768]{0:T(1024)S(1)}, s32[32768]{0:T(1024)}, u32[]{:S(2)}) copy-start(s32[32768]{0:T(1024)} %param.18) | copy-start | bytes 393220
  432.3 1.9 copy-start.5
  442.9 1.9 copy-start.5
  453.5 1.9 copy-start.5
  464.1 1.9 copy-start.5
  474.7 1.9 copy-start.5
  485.3 1.9 copy-start.5
  495.9 1.9 copy-start.5
  506.5 1.9 copy-start.5
  570.1 7.3 copy-start.1
  591.3 1.9 copy-start
  594.1 7.3 copy-start.1
  615.3 1.9 copy-start
  618.1 7.3 copy-start.1
  642.1 7.3 copy-start.1
  666.1 7.3 copy-start.1
  690.1 7.3 copy-start.1
  714.1 7.3 copy-start.1
  738.1 7.3 copy-start.1
  754.0 94.5 %copy-start.10 = (f32[256]{0:T(256)}, f32[256]{0:T(256)S(1)}, u32[]{:S(2)}) copy-start(f32[256]{0:T(256)S(1)} %get-tuple-element.1079) | copy-start | bytes 3076
  (8 other events, 13.2 us)
Sparse Core Ops, SparseCore 0:
  755.0 90.7 all-reduce.2
